TPU v7x, 32 devices: a whole 2x2x4 slice. The times are simulated.
32 devices in a mesh: snap: 8 (over z, y), ord: 4 (over x, core).
Axes of the slice: x: 2, y: 2, z: 4, core: 2. Of those that a mesh axis runs over, the one named last changes fastest.
Arguments:
- images: bfloat16 [512, 256, 1024], P(('snap', 'ord')), may hold values from -8 to 8
- cycle_masks: int32 [512, 256], P('snap'), may hold values from 0 to 1, as said below
- weights: float32 [512], P('snap'), may hold values from 1 to 4
- inversion: float32 [128, 128], replicated, may hold values from -1 to 2
Outputs:
- kam: float32 [128, 256, 256], P('ord', 'snap')
Inputs may be any that keep to these rules, and one draw needn't show every extreme that they name: `cycle_masks`: each entry is 0 or 1; the same 4 cycles, drawn from the seed, are 0 in every snapshot.
All inputs are finite; a program needn't handle non-finite values.
Results may differ from a plain program's by a relative error of at most 0.0015.
Values may be sent and summed in bfloat16 or wider, within the bound.
No kernel may reach another device: no remote copies, remote signals or barrier semaphores. Data moves between devices by JAX's collectives and lax.ppermute only.
A program may use at most 64 MiB of HBM per device.

v0:
```python
import math
import jax
import jax.numpy as jnp
from jax import lax
from jax.sharding import PartitionSpec as P


def make_table(orders, angles):
    order_index = jnp.arange(orders, dtype=jnp.int32)
    angle_index = jnp.arange(angles, dtype=jnp.int32)
    phase_index = order_index[:, None] * angle_index[None, :] % angles
    radians = phase_index.astype(jnp.float32) * (2.0 * math.pi / angles)
    norming = math.sqrt(2.0 / angles)
    return jnp.concatenate(
        [jnp.cos(radians) * norming, -jnp.sin(radians) * norming], axis=0
    ).astype(jnp.bfloat16)


def weighted_gram(arrived, weight_rows):
    weighted = (arrived.astype(jnp.float32) * weight_rows[None, None, :, None]).astype(jnp.bfloat16)
    return jnp.einsum("rlsq,rlsp->lqp", weighted, arrived, preferred_element_type=jnp.float32)


def on_device(images, cycle_masks, weights, inversion):
    snap_dev, cycle_count, angles = images.shape
    orders = inversion.shape[0]
    snap_size = lax.axis_size("snap")
    ord_size = lax.axis_size("ord")
    ord_index = lax.axis_index("ord")
    dft_table = make_table(orders, angles)
    group_masks = cycle_masks.astype(jnp.float32)
    own_masks = lax.dynamic_slice_in_dim(group_masks, ord_index * snap_dev, snap_dev, 0)
    coeffs = jnp.einsum("ka,sqa->ksq", dft_table, images, preferred_element_type=jnp.float32)
    coeffs = (
        (coeffs * own_masks[None]).astype(jnp.bfloat16).reshape(2, orders, snap_dev, cycle_count)
    )
    masked_weight = group_masks * weights[:, None]
    partial_count = jnp.einsum(
        "sq,sp->qp", masked_weight, group_masks, precision=lax.Precision.HIGHEST
    )
    per_device = orders // (snap_size * ord_size)
    shaped = coeffs.reshape(2, ord_size, snap_size * per_device, snap_dev, cycle_count)
    arrived = lax.all_to_all(
        lax.all_to_all(shaped, "snap", split_axis=2, concat_axis=3, tiled=True),
        "ord",
        split_axis=1,
        concat_axis=3,
        tiled=True,
    )
    arrived = arrived.reshape(2, per_device, -1, cycle_count)
    weight_all = lax.all_gather(weights, "snap", axis=0, tiled=True)
    weight_all = weight_all.reshape(snap_size, ord_size, snap_dev).transpose(1, 0, 2).reshape(-1)
    partial_value = weighted_gram(arrived, weight_all)
    gram_sum = lax.all_to_all(partial_value, "snap", split_axis=1, concat_axis=0, tiled=True)
    pair_count = lax.psum_scatter(partial_count, "snap", scatter_dimension=0, tiled=True)
    correl = gram_sum / jnp.maximum(pair_count, 1.0)[None]
    local_orders = correl.shape[0]
    own_rows = lax.dynamic_slice_in_dim(inversion, ord_index * local_orders, local_orders, 0)
    return jnp.einsum(
        "ln,nqp->lqp",
        own_rows,
        lax.all_gather(correl, "ord", axis=0, tiled=True),
        precision=lax.Precision.HIGHEST,
    )


def solution(mesh):
    placed = (P(("snap", "ord"), None, None), P("snap", None), P("snap"), P())
    return jax.shard_map(
        on_device, mesh=mesh, in_specs=placed, out_specs=P("ord", "snap", None), check_vma=False
    )
```

profile of v0, /device:TPU:0, one launch (start us, length us, event | category | flops | bytes accessed | tf_op | source)
XLA Modules:
  0.0 228.0 jit_solution(37374247902323197)
XLA Ops:
  6.5 2.2 multiply_convert_fusion.5
  8.7 0.8 convert_element_type.19
  9.6 5.8 %multiply_convert_fusion.1 = bf16[256,16,256]{2,0,1:T(8,128)(2,1)S(1)} fusion(bf16[16,256,1024]{2,1,0:T(8,128)(2,1)} %param.4, f32[16,256]{1,0:T(8,128)S(1)} %constant_dynamic-slice_fusion, bf16[128,1024]{1,0:T(8,128)(2,1)S(1)} %get-tuple-element.5, bf16[128,1024]{1,0:T(8,128)(2,1)S(1)} %get-tuple-element.6), kind=kOutput, calls=%fused_computation.1 | convolution fusion | flops 2150629376 | bytes 11026432 | tf_op jit(solution)/shard_map/ka,sqa->ksq/dot_general | solution.py:33
  15.3 1.6 copy.18
  17.0 55.3 %all_to_all.51 = bf16[2,4,32,16,256]{4,1,0,3,2:T(4,128)(2,1)S(1)} all-to-all(bf16[2,4,32,16,256]{4,1,0,3,2:T(4,128)(2,1)S(1)} %copy.18), channel_id=1, replica_groups=mesh['snap'=8,'ord'=4] {'snap'}, dimensions={2} | all-to-all | bytes 4194304 | tf_op jit(solution)/shard_map/all_to_all | solution.py:44
  72.3 1.8 copy.19
  74.1 3.6 %all-to-all-start.1 = ((bf16[2,4,4,128,256]{4,3,0,2,1:T(8,128)(2,1)}), bf16[2,4,4,128,256]{4,3,0,2,1:T(8,128)(2,1)S(1)}, u32[]{:S(2)}, u32[]{:S(2)}) async-start(bf16[2,4,4,128,256]{4,3,0,2,1:T(8,128)(2,1)} %bitcast.31), calls=%async_computation.1 | async-start | bytes 4194304 | tf_op jit(solution)/shard_map/all_to_all | solution.py:43
  77.8 0.6 dynamic-slice
  79.0 0.2 dynamic-update-slice
  79.3 19.4 %all-reduce = f32[512]{0:T(512)S(1)} all-reduce(f32[512]{0:T(512)S(1)} %dynamic-update-slice), channel_id=1, replica_groups=mesh['snap'=8,'ord'=4] {'snap'}, use_global_device_ids=true, to_apply=%add | all-reduce | flops 512 | bytes 4096
  98.9 4.5 %all-to-all-done.1 = bf16[2,4,4,128,256]{4,3,0,2,1:T(8,128)(2,1)S(1)} async-done(((bf16[2,4,4,128,256]{4,3,0,2,1:T(8,128)(2,1)}), bf16[2,4,4,128,256]{4,3,0,2,1:T(8,128)(2,1)S(1)}, u32[]{:S(2)}, u32[]{:S(2)}) %all-to-all-start.1) | async-done | bytes 2097184 | tf_op jit(solution)/shard_map/all_to_all | solution.py:43
  103.4 0.1 copy.20
  103.5 1.2 fusion.2
  104.8 1.6 copy.23
  106.4 3.6 %all-to-all-start.2 = ((f32[4,256,256]{2,0,1:T(4,128)}), f32[4,256,256]{2,0,1:T(4,128)S(1)}, u32[]{:S(2)}, u32[]{:S(2)}) async-start(f32[4,256,256]{2,0,1:T(4,128)} %copy.23), calls=%async_computation.2 | async-start | bytes 2097152 | tf_op jit(solution)/shard_map/all_to_all | solution.py:54
  110.1 1.2 fusion.11
  111.3 68.1 %reduce-scatter.2.cloned.1.call-done = f32[32,256]{1,0:T(8,128)} async-done(((f32[256,256]{1,0:T(8,128)}), f32[32,256]{1,0:T(8,128)}) %reduce-scatter.2.cloned.1.call-update) | async-done | bytes 32784 | tf_op jit(solution)/shard_map/reduce_scatter | solution.py:55
  179.4 0.8 broadcast_maximum_fusion
  180.2 0.3 copy.29
  180.5 0.4 all_to_all.47
  180.9 1.1 broadcast_divide_fusion
  182.0 33.6 %all-gather.2.cloned.1.call-done = f32[128,32,256]{2,0,1:T(8,128)} async-done(((f32[32,32,256]{2,0,1:T(8,128)}), f32[128,32,256]{2,0,1:T(8,128)}) %all-gather.2.cloned.1.call-update) | async-done | bytes 4194320 | tf_op jit(solution)/shard_map/all_gather | solution.py:62
  215.6 4.0 %fusion.14 = f32[32,32,256]{2,0,1:T(8,128)S(1)} fusion(f32[128,32,256]{2,0,1:T(8,128)} %all-gather.2.cloned.1.call-done, f32[128,128]{1,0:T(8,128)S(1)} %copy-done, s32[]{:T(128)S(6)} %select_n.15), kind=kOutput, calls=%fused_computation.24 | convolution fusion | flops 402653184 | bytes 5259268 | tf_op jit(solution)/shard_map/ln,nqp->lqp/dot_general | solution.py:59
  219.6 1.6 copy.25
  (18 shorter events, 0.3 us)
Async XLA Ops:
  6.5 209.1 %copy-start = (f32[128,128]{1,0:T(8,128)S(1)}, f32[128,128]{1,0:T(8,128)}, u32[]{:S(2)}) copy-start(f32[128,128]{1,0:T(8,128)} %param.7) | copy-start | bytes 196612
  72.3 5.4 %copy-start.3 = (u32[32]{0:T(128)S(1)}, u32[32]{0:T(128)}, u32[]{:S(2)}) copy-start(u32[32]{0:T(128)} %constant.37) | copy-start | bytes 388
  72.3 6.7 %copy-start.2 = (f32[64]{0:T(128)S(1)}, f32[64]{0:T(128)}, u32[]{:S(2)}) copy-start(f32[64]{0:T(128)} %param.6) | copy-start | bytes 772
  74.1 29.2 %all-to-all-start.1 = ((bf16[2,4,4,128,256]{4,3,0,2,1:T(8,128)(2,1)}), bf16[2,4,4,128,256]{4,3,0,2,1:T(8,128)(2,1)S(1)}, u32[]{:S(2)}, u32[]{:S(2)}) async-start(bf16[2,4,4,128,256]{4,3,0,2,1:T(8,128)(2,1)} %bitcast.31), calls=%async_computation.1 | async-start | bytes 4194304 | tf_op jit(solution)/shard_map/all_to_all | solution.py:43
  103.5 6.5 %copy-start.1 = (s32[64,256]{1,0:T(8,128)S(1)}, s32[64,256]{1,0:T(8,128)}, u32[]{:S(2)}) copy-start(s32[64,256]{1,0:T(8,128)} %param.5) | copy-start | bytes 196612
  106.4 73.8 %all-to-all-start.2 = ((f32[4,256,256]{2,0,1:T(4,128)}), f32[4,256,256]{2,0,1:T(4,128)S(1)}, u32[]{:S(2)}, u32[]{:S(2)}) async-start(f32[4,256,256]{2,0,1:T(4,128)} %copy.23), calls=%async_computation.2 | async-start | bytes 2097152 | tf_op jit(solution)/shard_map/all_to_all | solution.py:54
  110.0 69.4 %reduce-scatter.2.cloned.1.call-start = ((), (), s32[]{:S(2)}) async-start(), calls=%async_computation.4 | async-start | bytes 294912 | tf_op jit(solution)/shard_map/reduce_scatter | solution.py:55
  111.3 104.3 %all-gather.2.cloned.1.call-start = ((), (), s32[]{:S(2)}) async-start(), calls=%async_computation.5 | async-start | bytes 5242880 | tf_op jit(solution)/shard_map/all_gather | solution.py:62
Sparse Core Ops, SparseCore 0:
  114.1 65.2 reduce-scatter.1
  182.1 33.4 all-gather.1
where the time goes:
time: 228 us
  waiting for transfers between devices  106 us (46%)
  blocking collectives  74.8 us (33%)
  between operations  14.2 us (6%)
  matrix products  12.1 us (5%)
  local copies, waits for them, and re-layouts  8.48 us (4%)
  starting transfers between devices  7.28 us (3%)
  other arithmetic  4.87 us (2%)
    reduce_scatter x1, waiting for transfers between devices, on_device(): lax.psum_scatter(partial_count, 'snap', scatter_dimension=0, tiled=True)  68.1 us
    all_to_all x1, blocking collectives, on_device(): lax.all_to_all(shaped, 'snap', split_axis=2, concat_axis=3, tiled=True)  55.3 us
    all_gather x1, waiting for transfers between devices, on_device(): lax.all_gather(correl, 'ord', axis=0, tiled=True)  33.6 us
    unnamed x1, blocking collectives  19.4 us
    dot_general x1, matrix products, on_device(): jnp.einsum('ka,sqa->ksq', dft_table, images, preferred_element_type=jnp.f...  5.75 us
  transfers between devices with their start and end apart: 4, of which 3 were waited for; matrix products, arithmetic and copies ran while one was open for 1% of the time, Pallas kernels for 0%

commit v1 on v0

--- a/solution.py
+++ b/solution.py
@@ -41,7 +41,12 @@
     per_device = orders // (snap_size * ord_size)
     shaped = coeffs.reshape(2, ord_size, snap_size * per_device, snap_dev, cycle_count)
     arrived = lax.all_to_all(
-        lax.all_to_all(shaped, "snap", split_axis=2, concat_axis=3, tiled=True),
+        jnp.concatenate(
+            lax.all_to_all(
+                jnp.stack(jnp.split(shaped, lax.axis_size("snap"), axis=2)), "snap", 0, 0
+            ),
+            axis=3,
+        ),
         "ord",
         split_axis=1,
         concat_axis=3,

time: 228 us -> 229 us (level)
    reshape x0 -> x1, local copies, waits for them, and re-layouts: none -> 2.53 us  [on_device(): jnp.concatenate(lax.all_to_all(jnp.stack(jnp.split(shaped, lax.axis_size(...]
where the time goes in v1:
time: 229 us
  waiting for transfers between devices  106 us (46%)
  blocking collectives  74.8 us (33%)
  between operations  14.2 us (6%)
  matrix products  12.1 us (5%)
  local copies, waits for them, and re-layouts  8.82 us (4%)
  starting transfers between devices  7.41 us (3%)
  other arithmetic  4.87 us (2%)
    reduce_scatter x1, waiting for transfers between devices, on_device(): lax.psum_scatter(partial_count, 'snap', scatter_dimension=0, tiled=True)  68.1 us
    all_to_all x1, blocking collectives, on_device(): lax.all_to_all(jnp.stack(jnp.split(shaped, lax.axis_size('snap'), axis=2)...  55.3 us
    all_gather x1, waiting for transfers between devices, on_device(): lax.all_gather(correl, 'ord', axis=0, tiled=True)  33.6 us
    unnamed x1, blocking collectives  19.4 us
    dot_general x1, matrix products, on_device(): jnp.einsum('ka,sqa->ksq', dft_table, images, preferred_element_type=jnp.f...  5.75 us
  transfers between devices with their start and end apart: 4, of which 3 were waited for; matrix products, arithmetic and copies ran while one was open for 1% of the time, Pallas kernels for 0%

profile of v1, /device:TPU:0, one launch (start us, length us, event | category | flops | bytes accessed | tf_op | source)
XLA Modules:
  0.0 228.5 jit_solution(10686810832674885047)
XLA Ops:
  6.5 2.2 multiply_convert_fusion.5
  8.7 0.8 convert_element_type.19
  9.6 5.8 %multiply_convert_fusion.1 = bf16[256,16,256]{2,0,1:T(8,128)(2,1)S(1)} fusion(bf16[16,256,1024]{2,1,0:T(8,128)(2,1)} %param.4, f32[16,256]{1,0:T(8,128)S(1)} %constant_dynamic-slice_fusion, bf16[128,1024]{1,0:T(8,128)(2,1)S(1)} %get-tuple-element.5, bf16[128,1024]{1,0:T(8,128)(2,1)S(1)} %get-tuple-element.6), kind=kOutput, calls=%fused_computation.1 | convolution fusion | flops 2150629376 | bytes 11026432 | tf_op jit(solution)/shard_map/ka,sqa->ksq/dot_general | solution.py:33
  15.8 0.2 fusion.15
  16.1 0.2 fusion.13
  16.6 55.3 %all_to_all.38 = bf16[8,2,4,4,16,256]{5,3,2,1,4,0:T(4,128)(2,1)S(1)} all-to-all(bf16[8,2,4,4,16,256]{5,3,2,1,4,0:T(4,128)(2,1)S(1)} %fusion.11), channel_id=1, replica_groups=mesh['snap'=8,'ord'=4] {'snap'}, dimensions={0} | all-to-all | bytes 4194304 | tf_op jit(solution)/shard_map/all_to_all | solution.py:45
  72.0 2.5 %copy.18 = bf16[2,4,4,8,16,256]{5,4,3,0,2,1:T(8,128)(2,1)} copy(bf16[2,4,4,8,16,256]{5,2,1,0,4,3:T(4,128)(2,1)S(1)} %bitcast.62) | data formatting | bytes 4194304 | tf_op jit(solution)/shard_map/reshape | solution.py:44
  74.5 3.7 %all-to-all-start.1 = ((bf16[2,4,4,128,256]{4,3,0,2,1:T(8,128)(2,1)}), bf16[2,4,4,128,256]{4,3,0,2,1:T(8,128)(2,1)S(1)}, u32[]{:S(2)}, u32[]{:S(2)}) async-start(bf16[2,4,4,128,256]{4,3,0,2,1:T(8,128)(2,1)} %bitcast.61), calls=%async_computation.1 | async-start | bytes 4194304 | tf_op jit(solution)/shard_map/all_to_all | solution.py:43
  78.3 0.6 dynamic-slice
  79.5 0.2 dynamic-update-slice
  79.8 19.4 %all-reduce = f32[512]{0:T(512)S(1)} all-reduce(f32[512]{0:T(512)S(1)} %dynamic-update-slice), channel_id=1, replica_groups=mesh['snap'=8,'ord'=4] {'snap'}, use_global_device_ids=true, to_apply=%add | all-reduce | flops 512 | bytes 4096
  99.4 4.5 %all-to-all-done.1 = bf16[2,4,4,128,256]{4,3,0,2,1:T(8,128)(2,1)S(1)} async-done(((bf16[2,4,4,128,256]{4,3,0,2,1:T(8,128)(2,1)}), bf16[2,4,4,128,256]{4,3,0,2,1:T(8,128)(2,1)S(1)}, u32[]{:S(2)}, u32[]{:S(2)}) %all-to-all-start.1) | async-done | bytes 2097184 | tf_op jit(solution)/shard_map/all_to_all | solution.py:43
  104.0 1.2 fusion.2
  105.3 1.6 copy.22
  106.9 3.6 %all-to-all-start.2 = ((f32[4,256,256]{2,0,1:T(4,128)}), f32[4,256,256]{2,0,1:T(4,128)S(1)}, u32[]{:S(2)}, u32[]{:S(2)}) async-start(f32[4,256,256]{2,0,1:T(4,128)} %copy.22), calls=%async_computation.2 | async-start | bytes 2097152 | tf_op jit(solution)/shard_map/all_to_all | solution.py:59
  110.6 1.2 fusion.19
  111.8 68.1 %reduce-scatter.2.cloned.1.call-done = f32[32,256]{1,0:T(8,128)} async-done(((f32[256,256]{1,0:T(8,128)}), f32[32,256]{1,0:T(8,128)}) %reduce-scatter.2.cloned.1.call-update) | async-done | bytes 32784 | tf_op jit(solution)/shard_map/reduce_scatter | solution.py:60
  180.0 0.8 broadcast_maximum_fusion
  180.7 0.3 copy.28
  181.0 0.4 all_to_all.34
  181.4 1.1 broadcast_divide_fusion
  182.5 33.6 %all-gather.2.cloned.1.call-done = f32[128,32,256]{2,0,1:T(8,128)} async-done(((f32[32,32,256]{2,0,1:T(8,128)}), f32[128,32,256]{2,0,1:T(8,128)}) %all-gather.2.cloned.1.call-update) | async-done | bytes 4194320 | tf_op jit(solution)/shard_map/all_gather | solution.py:67
  216.1 4.0 %fusion.22 = f32[32,32,256]{2,0,1:T(8,128)S(1)} fusion(f32[128,32,256]{2,0,1:T(8,128)} %all-gather.2.cloned.1.call-done, f32[128,128]{1,0:T(8,128)S(1)} %copy-done, s32[]{:T(128)S(6)} %select_n.15), kind=kOutput, calls=%fused_computation.40 | convolution fusion | flops 402653184 | bytes 5259268 | tf_op jit(solution)/shard_map/ln,nqp->lqp/dot_general | solution.py:64
  220.1 1.6 copy.24
  (25 shorter events, 1.4 us)
Async XLA Ops:
  6.5 209.6 %copy-start = (f32[128,128]{1,0:T(8,128)S(1)}, f32[128,128]{1,0:T(8,128)}, u32[]{:S(2)}) copy-start(f32[128,128]{1,0:T(8,128)} %param.7) | copy-start | bytes 196612
  74.5 3.8 %copy-start.3 = (u32[32]{0:T(128)S(1)}, u32[32]{0:T(128)}, u32[]{:S(2)}) copy-start(u32[32]{0:T(128)} %constant.37) | copy-start | bytes 388
  74.5 5.0 %copy-start.2 = (f32[64]{0:T(128)S(1)}, f32[64]{0:T(128)}, u32[]{:S(2)}) copy-start(f32[64]{0:T(128)} %param.6) | copy-start | bytes 772
  74.5 29.4 %all-to-all-start.1 = ((bf16[2,4,4,128,256]{4,3,0,2,1:T(8,128)(2,1)}), bf16[2,4,4,128,256]{4,3,0,2,1:T(8,128)(2,1)S(1)}, u32[]{:S(2)}, u32[]{:S(2)}) async-start(bf16[2,4,4,128,256]{4,3,0,2,1:T(8,128)(2,1)} %bitcast.61), calls=%async_computation.1 | async-start | bytes 4194304 | tf_op jit(solution)/shard_map/all_to_all | solution.py:43
  105.3 5.3 %copy-start.1 = (s32[64,256]{1,0:T(8,128)S(1)}, s32[64,256]{1,0:T(8,128)}, u32[]{:S(2)}) copy-start(s32[64,256]{1,0:T(8,128)} %param.5) | copy-start | bytes 196612
  106.9 73.8 %all-to-all-start.2 = ((f32[4,256,256]{2,0,1:T(4,128)}), f32[4,256,256]{2,0,1:T(4,128)S(1)}, u32[]{:S(2)}, u32[]{:S(2)}) async-start(f32[4,256,256]{2,0,1:T(4,128)} %copy.22), calls=%async_computation.2 | async-start | bytes 2097152 | tf_op jit(solution)/shard_map/all_to_all | solution.py:59
  110.5 69.4 %reduce-scatter.2.cloned.1.call-start = ((), (), s32[]{:S(2)}) async-start(), calls=%async_computation.4 | async-start | bytes 294912 | tf_op jit(solution)/shard_map/reduce_scatter | solution.py:60
  111.8 104.3 %all-gather.2.cloned.1.call-start = ((), (), s32[]{:S(2)}) async-start(), calls=%async_computation.5 | async-start | bytes 5242880 | tf_op jit(solution)/shard_map/all_gather | solution.py:67
Sparse Core Ops, SparseCore 0:
  114.7 65.2 reduce-scatter.1
  182.6 33.4 all-gather.1
